TPU v7x, 512 devices: a whole 4x4x16 slice. The times are simulated.
512 devices in a mesh: row: 32 (over y, z_hi, x), col: 16 (over z_lo, core).
Axes of the slice: x: 4, y: 4, z: 16 (z_hi: 2, z_lo: 8; z = z_hi * 8 + z_lo), core: 2. Of those that a mesh axis runs over, the one named last changes fastest.
Arguments:
- query_field: bfloat16 [512, 256, 1152], P('row', 'col'), may hold values from -136 to 136
- key_field: bfloat16 [512, 256, 1152], P('row', 'col'), may hold values from -8.5 to 8.5
- value_field: bfloat16 [512, 256, 1152], P('row', 'col'), may hold values from -6 to 6
- query_tan: bfloat16 [512, 256, 1152], P('row', 'col'), may hold values from -6 to 6
- key_tan: bfloat16 [512, 256, 1152], P('row', 'col'), may hold values from -6 to 6
- value_tan: bfloat16 [512, 256, 1152], P('row', 'col'), may hold values from -6 to 6
- pool_near: float32 [4, 4], replicated, may hold values from -1.5 to 1.5
- pool_far: float32 [16, 16], replicated, may hold values from -0.375 to 0.375
- level_bias: float32 [2, 16], replicated, may hold values from 0.5 to 2.5
Outputs:
- mixed: bfloat16 [512, 256, 1152], P('row', 'col')
- mixed_tan: bfloat16 [512, 256, 1152], P('row', 'col')
All inputs are finite; a program needn't handle non-finite values.
Results may differ from a plain program's by a relative error of at most 0.012.
Values may be sent and summed in bfloat16 or wider, within the bound.
A program may use at most 128 MiB of HBM per device.

v0:
```python
import jax
import jax.numpy as jnp
from jax import lax
from jax.sharding import PartitionSpec as P

HEADS = 16
RIM = 8
NEAR_POOL = 4


def with_halo(cells, sides, width):
    for axis, dim in sides:
        count = lax.axis_size(axis)
        ends = count - 1
        head = lax.slice_in_dim(cells, 0, width, axis=dim)
        tail = lax.slice_in_dim(cells, cells.shape[dim] - width, cells.shape[dim], axis=dim)
        cells = jnp.concatenate(
            [
                lax.ppermute(tail, axis, [(i, (i + 1) % count) for i in range(ends)]),
                cells,
                lax.ppermute(head, axis, [((i + 1) % count, i) for i in range(ends)]),
            ],
            axis=dim,
        )
    return cells


def partner(block, axis, stride):
    count = lax.axis_size(axis)
    route = []
    for low in range(count):
        high = low | 1 << stride
        if high != low and high < count:
            route += [(low, high), (high, low)]
    return lax.ppermute(block, axis, route)


def pool_stack(stacked_wide, weights, size):
    count, row_count, col_count, width = stacked_wide.shape
    blocks = stacked_wide.reshape(count, row_count // size, size, col_count // size, size, width)
    pooled = jnp.einsum("napbqd,pq->nabd", blocks, weights, precision=lax.Precision.HIGHEST)
    return pooled.astype(jnp.bfloat16).reshape(count, -1, width)


def body(
    query_field,
    key_field,
    value_field,
    query_tan,
    key_tan,
    value_tan,
    pool_near,
    pool_far,
    level_bias,
):
    window = query_field.shape[0]
    width = query_field.shape[2]
    head_dim = width // HEADS
    pair_width = 2 * head_dim
    token_count = window * window
    score_scale = head_dim ** (-0.5)
    stacked = jnp.stack([key_field, value_field, key_tan, value_tan], 0)
    extended = with_halo(stacked, (("row", 1), ("col", 2)), RIM)
    span = window + 2 * RIM
    fine_keys = extended.reshape(4, span * span, width)
    stacked_wide = stacked.astype(jnp.float32)
    near_local = pool_stack(stacked_wide, pool_near, NEAR_POOL)
    near_pair = jnp.concatenate([near_local, partner(near_local, "row", 0)], axis=1)
    near_keys = jnp.concatenate([near_pair, partner(near_pair, "col", 0)], axis=1)
    far_local = pool_stack(stacked_wide, pool_far, window)
    col_done = lax.all_gather(far_local, "col", axis=1, tiled=True)
    far_keys = lax.all_gather(col_done, "row", axis=1, tiled=True)
    row_ids = lax.axis_index("row") * window - RIM + jnp.arange(span, dtype=jnp.int32)
    col_ids = lax.axis_index("col") * window - RIM + jnp.arange(span, dtype=jnp.int32)
    row_ok = (row_ids >= 0) & (row_ids < window * lax.axis_size("row"))
    col_ok = (col_ids >= 0) & (col_ids < window * lax.axis_size("col"))
    valid = (row_ok[:, None] & col_ok[None, :]).reshape(span * span)
    query_flat = query_field.reshape(token_count, width)
    qtan_flat = query_tan.reshape(token_count, width)
    blocks = (fine_keys, near_keys, far_keys)

    def pair_step(group, carry):
        out_acc, tan_acc = carry
        start = group * pair_width

        def columns(array):
            return lax.dynamic_slice_in_dim(array, start, pair_width, array.ndim - 1)

        query_pair = columns(query_flat).reshape(token_count, 2, head_dim)
        qtan_pair = columns(qtan_flat).reshape(token_count, 2, head_dim)
        bias_pair = lax.dynamic_slice_in_dim(level_bias, group * 2, 2, 1)
        score_parts = []
        tangent_parts = []
        value_parts = []
        valtan_parts = []
        for level, block in enumerate(blocks):
            count = block.shape[1]
            key_part = columns(block[0]).reshape(count, 2, head_dim)
            keytan_part = columns(block[2]).reshape(count, 2, head_dim)
            value_parts.append(columns(block[1]).reshape(count, 2, head_dim))
            valtan_parts.append(columns(block[3]).reshape(count, 2, head_dim))
            level_scores = (
                jnp.einsum("qhd,khd->hqk", query_pair, key_part, preferred_element_type=jnp.float32)
                * score_scale
            )
            if level == 0:
                level_scores = jnp.where(valid[None, None, :], level_scores, jnp.float32(-jnp.inf))
            else:
                level_scores = level_scores + bias_pair[level - 1][:, None, None]
            score_parts.append(level_scores)
            tangent_parts.append(
                (
                    jnp.einsum(
                        "qhd,khd->hqk", qtan_pair, key_part, preferred_element_type=jnp.float32
                    )
                    + jnp.einsum(
                        "qhd,khd->hqk", query_pair, keytan_part, preferred_element_type=jnp.float32
                    )
                )
                * score_scale
            )
        top = jnp.max(score_parts[0], axis=-1, keepdims=True)
        for level in range(1, 3):
            top = jnp.maximum(top, jnp.max(score_parts[level], axis=-1, keepdims=True))
        total = jnp.zeros_like(top)
        for level in range(3):
            total = total + jnp.sum(jnp.exp(score_parts[level] - top), axis=-1, keepdims=True)
        row_total = jnp.zeros((2, token_count), jnp.float32)
        mix = jnp.zeros((token_count, 2, head_dim), jnp.float32)
        mix_extra = jnp.zeros((token_count, 2, head_dim), jnp.float32)
        for level in range(3):
            weights = jnp.exp(score_parts[level] - top) / total
            product = weights * tangent_parts[level]
            row_total = row_total + jnp.sum(product, axis=-1)
            weight_part = weights.astype(jnp.bfloat16)
            product_part = product.astype(jnp.bfloat16)
            mix = mix + jnp.einsum(
                "hqk,khd->qhd", weight_part, value_parts[level], preferred_element_type=jnp.float32
            )
            mix_extra = mix_extra + jnp.einsum(
                "hqk,khd->qhd", product_part, value_parts[level], preferred_element_type=jnp.float32
            )
            mix_extra = mix_extra + jnp.einsum(
                "hqk,khd->qhd", weight_part, valtan_parts[level], preferred_element_type=jnp.float32
            )
        mix_tan = mix_extra - jnp.transpose(row_total)[:, :, None] * mix
        out_acc = lax.dynamic_update_slice_in_dim(
            out_acc, mix.reshape(token_count, pair_width).astype(jnp.bfloat16), start, 1
        )
        tan_acc = lax.dynamic_update_slice_in_dim(
            tan_acc, mix_tan.reshape(token_count, pair_width).astype(jnp.bfloat16), start, 1
        )
        return (out_acc, tan_acc)

    empty = jnp.zeros((token_count, width), jnp.bfloat16)
    mixed, mixed_tan = lax.fori_loop(0, HEADS // 2, pair_step, (empty, empty))
    return (mixed.reshape(window, window, width), mixed_tan.reshape(window, window, width))


def solution(mesh):
    in_specs = (
        P("row", "col", None),
        P("row", "col", None),
        P("row", "col", None),
        P("row", "col", None),
        P("row", "col", None),
        P("row", "col", None),
        P(),
        P(),
        P(),
    )
    out_specs = (P("row", "col", None), P("row", "col", None))
    return jax.shard_map(body, mesh=mesh, in_specs=in_specs, out_specs=out_specs, check_vma=False)
```

profile of v0, /device:TPU:96, one launch (start us, length us, event | category | flops | bytes accessed | tf_op | source)
XLA Modules:
  0.0 478.5 jit_solution(2326812249168049933)
XLA Ops:
  10.9 4.6 collective-permute-start
  17.8 21.2 %all-gather = bf16[4,18432]{1,0:T(4,128)(2,1)S(1)} all-gather(bf16[4,1152]{1,0:T(4,128)(2,1)S(1)} %bitcast.210), channel_id=2, replica_groups=mesh['row'=32,'col'=16] {'col'}, dimensions={1}, use_global_device_ids=true | all-gather | bytes 156672 | tf_op jit(solution)/shard_map/all_gather | solution.py:71
  39.9 5.1 %collective-permute-done.1 = bf16[4,8,16,1152]{3,2,1,0:T(8,128)(2,1)} collective-permute-done((bf16[4,8,16,1152]{3,2,1,0:T(8,128)(2,1)}, bf16[4,8,16,1152]{3,2,1,0:T(8,128)(2,1)}, u32[]{:S(2)}, u32[]{:S(2)}) %collective-permute-start.1) | collective-permute-done | bytes 1179680 | tf_op jit(solution)/shard_map/ppermute | solution.py:21
  45.1 2.8 pad_maximum_fusion.1
  47.9 2.6 fusion.55
  52.5 3.7 collective-permute-start.3
  58.4 3.6 fusion.44
  62.1 4.6 collective-permute-start.4
  66.8 4.4 collective-permute-done.4
  74.6 2.1 copy.25
  77.9 3.2 collective-permute-done.2
  82.9 9.8 %pad_maximum_fusion = bf16[4,32,32,1152]{3,2,1,0:T(8,128)(2,1)} fusion(bf16[4,32,8,1152]{3,2,1,0:T(8,128)(2,1)} %collective-permute-done.3, bf16[4,8,16,1152]{3,2,1,0:T(8,128)(2,1)} %collective-permute-done.1, bf16[1,16,16,1152]{3,2,1,0:T(8,128)(2,1)S(1)} %bitcast.188, bf16[1,16,16,1152]{3,2,1,0:T(8,128)(2,1)S(1)} %bitcast.191, ...), kind=kLoop, calls=%fused_computation.75 | loop fusion | flops 75497472 | bytes 18874368 | tf_op jit(solution)/shard_map/concatenate | solution.py:17
  92.6 12.6 %copy.22 = bf16[4,1024,1152]{1,2,0:T(8,128)(2,1)} copy(bf16[4,1024,1152]{2,1,0:T(8,128)(2,1)} %bitcast.169) | data formatting | bytes 18874368
  105.3 228.3 %all-gather.3.cloned.1.call-done = bf16[4,512,1152]{2,1,0:T(8,128)(2,1)} async-done(((bf16[4,16,1152]{2,1,0:T(8,128)(2,1)}), bf16[4,512,1152]{2,1,0:T(8,128)(2,1)}) %all-gather.3.cloned.1.call-update) | async-done | bytes 4718608 | tf_op jit(solution)/shard_map/all_gather | solution.py:72
  333.5 6.7 %copy.24 = bf16[4,512,1152]{1,2,0:T(8,128)(2,1)} copy(bf16[4,512,1152]{2,1,0:T(8,128)(2,1)} %all-gather.3.cloned.1.call-done) | data formatting | bytes 9437184
  340.3 129.2 %while.16 = (s32[]{:T(128)}, bf16[256,1152]{0,1:T(8,128)(2,1)S(1)}, bf16[256,1152]{0,1:T(8,128)(2,1)S(1)}, bf16[4,1024,1152]{1,2,0:T(8,128)(2,1)}, bf16[256,1152...) while((s32[]{:T(128)}, bf16[256,1152]{0,1:T(8,128)(2,1)S(1)}, ...), condition=%wide.region_10.11_spmd.clone, body=%wide.region_0.10_spmd.clone.sunk | while | flops 726347264 | bytes 104430016 | solution.py:156
  342.6 2.8 fusion.181
  358.7 2.8 fusion.181
  374.9 2.8 fusion.181
  391.0 2.8 fusion.181
  407.2 2.8 fusion.181
  423.3 2.8 fusion.181
  439.5 2.8 fusion.181
  455.6 2.8 fusion.181
  (463 shorter events, 124.8 us)
Async XLA Ops:
  7.2 9.6 %copy-start = (f32[16,16]{1,0:T(8,128)S(1)}, f32[16,16]{1,0:T(8,128)}, u32[]{:S(2)}) copy-start(f32[16,16]{1,0:T(8,128)} %param.18) | copy-start | bytes 3076
  7.2 326.3 %all-gather.3.cloned.1.call-start = ((), (), s32[]{:S(2)}) async-start(), calls=%async_computation | async-start | bytes 4866048 | tf_op jit(solution)/shard_map/all_gather | solution.py:72
  10.8 34.2 %copy-start.3 = (bf16[16,16,1152]{2,1,0:T(8,128)(2,1)S(1)}, bf16[16,16,1152]{2,1,0:T(8,128)(2,1)}, u32[]{:S(2)}) copy-start(bf16[16,16,1152]{2,1,0:T(8,128)(2,1)} %param.16) | copy-start | bytes 1769476
  10.8 34.2 %copy-start.4 = (bf16[16,16,1152]{2,1,0:T(8,128)(2,1)S(1)}, bf16[16,16,1152]{2,1,0:T(8,128)(2,1)}, u32[]{:S(2)}) copy-start(bf16[16,16,1152]{2,1,0:T(8,128)(2,1)} %param.15) | copy-start | bytes 1769476
  10.9 34.2 %copy-start.5 = (bf16[16,16,1152]{2,1,0:T(8,128)(2,1)S(1)}, bf16[16,16,1152]{2,1,0:T(8,128)(2,1)}, u32[]{:S(2)}) copy-start(bf16[16,16,1152]{2,1,0:T(8,128)(2,1)} %param.13) | copy-start | bytes 1769476
  10.9 34.2 %copy-start.6 = (bf16[16,16,1152]{2,1,0:T(8,128)(2,1)S(1)}, bf16[16,16,1152]{2,1,0:T(8,128)(2,1)}, u32[]{:S(2)}) copy-start(bf16[16,16,1152]{2,1,0:T(8,128)(2,1)} %param.12) | copy-start | bytes 1769476
  10.9 29.1 %collective-permute-start = (bf16[4,8,16,1152]{3,2,1,0:T(8,128)(2,1)}, bf16[4,8,16,1152]{3,2,1,0:T(8,128)(2,1)}, u32[]{:S(2)}, u32[]{:S(2)}) collective-permute-start(bf16[4,8,16,1152]{3,2,1,0:T(8,128)(2,1)} %get-tuple-element.265), channel_id=1, source_target_pairs={{0,16},{16,32},{32,48},{48,64},{64,80},{80,96},{96,112},{112,128},... | collective-permute-start | bytes 3538952 | tf_op jit(solution)/shard_map/ppermute | solution.py:19
  15.4 29.6 %collective-permute-start.1 = (bf16[4,8,16,1152]{3,2,1,0:T(8,128)(2,1)}, bf16[4,8,16,1152]{3,2,1,0:T(8,128)(2,1)}, u32[]{:S(2)}, u32[]{:S(2)}) collective-permute-start(bf16[4,8,16,1152]{3,2,1,0:T(8,128)(2,1)} %get-tuple-element.266), channel_id=1, source_target_pairs={{16,0},{32,16},{48,32},{64,48},{80,64},{96,80},{112,96},{128,112},... | collective-permute-start | bytes 3538952 | tf_op jit(solution)/shard_map/ppermute | solution.py:21
  50.5 30.5 %collective-permute-start.2 = (bf16[4,32,8,1152]{3,2,1,0:T(8,128)(2,1)}, bf16[4,32,8,1152]{3,2,1,0:T(8,128)(2,1)}, u32[]{:S(2)}, u32[]{:S(2)}) collective-permute-start(bf16[4,32,8,1152]{3,2,1,0:T(8,128)(2,1)} %get-tuple-element.263), channel_id=1, source_target_pairs={{0,1},{1,2},{2,3},{3,4},{4,5},{5,6},{6,7},{7,8},{8,9},{9,10},{10,1... | collective-permute-start | bytes 7077896 | tf_op jit(solution)/shard_map/ppermute | solution.py:19
  52.5 5.9 %copy-start.10 = (f32[4,4]{1,0:T(4,128)S(1)}, f32[4,4]{1,0:T(4,128)}, u32[]{:S(2)}) copy-start(f32[4,4]{1,0:T(4,128)} %param.17) | copy-start | bytes 196
  52.5 30.4 %collective-permute-start.3 = (bf16[4,32,8,1152]{3,2,1,0:T(8,128)(2,1)}, bf16[4,32,8,1152]{3,2,1,0:T(8,128)(2,1)}, u32[]{:S(2)}, u32[]{:S(2)}) collective-permute-start(bf16[4,32,8,1152]{3,2,1,0:T(8,128)(2,1)} %get-tuple-element.264), channel_id=1, source_target_pairs={{1,0},{2,1},{3,2},{4,3},{5,4},{6,5},{7,6},{8,7},{9,8},{10,9},{11,1... | collective-permute-start | bytes 7077896 | tf_op jit(solution)/shard_map/ppermute | solution.py:21
  62.1 14.7 %copy-start.7 = (bf16[4,16,1152]{2,1,0:T(8,128)(2,1)}, bf16[4,16,1152]{2,1,0:T(8,128)(2,1)S(1)}, u32[]{:S(2)}) copy-start(bf16[4,16,1152]{2,1,0:T(8,128)(2,1)S(1)} %reshape.226) | copy-start | bytes 442372
  62.1 9.1 %collective-permute-start.4 = (bf16[4,16,1152]{2,1,0:T(8,128)(2,1)S(1)}, bf16[4,16,1152]{2,1,0:T(8,128)(2,1)S(1)}, u32[]{:S(2)}, u32[]{:S(2)}) collective-permute-start(bf16[4,16,1152]{2,1,0:T(8,128)(2,1)S(1)} %reshape.226), channel_id=1, source_target_pairs={{0,16},{16,0},{32,48},{48,32},{64,80},{80,64},{96,112},{112,96},{1... | collective-permute-start | bytes 442376 | tf_op jit(solution)/shard_map/ppermute | solution.py:35
  71.2 5.6 %copy-start.8 = (bf16[4,16,1152]{2,1,0:T(8,128)(2,1)}, bf16[4,16,1152]{2,1,0:T(8,128)(2,1)S(1)}, u32[]{:S(2)}) copy-start(bf16[4,16,1152]{2,1,0:T(8,128)(2,1)S(1)} %collective-permute-done.4) | copy-start | bytes 442372
  71.2 5.6 %collective-permute-start.5 = (bf16[4,32,1152]{2,1,0:T(8,128)(2,1)S(1)}, bf16[4,32,1152]{2,1,0:T(8,128)(2,1)}, u32[]{:S(2)}, u32[]{:S(2)}) collective-permute-start(bf16[4,32,1152]{2,1,0:T(8,128)(2,1)S(1)} %pad_maximum_fusion.8), channel_id=1, source_target_pairs={{0,1},{1,0},{2,3},{3,2},{4,5},{5,4},{6,7},{7,6},{8,9},{9,8},{10,11... | collective-permute-start | bytes 884744 | tf_op jit(solution)/shard_map/ppermute | solution.py:35
  105.3 235.0 %copy-start.9 = (f32[2,16]{1,0:T(2,128)S(1)}, f32[2,16]{1,0:T(2,128)}, u32[]{:S(2)}) copy-start(f32[2,16]{1,0:T(2,128)} %param.19) | copy-start | bytes 388
  342.6 5.1 %copy-start.2 = (bf16[4,1024,1152]{1,2,0:T(8,128)(2,1)S(1)}, bf16[4,1024,1152]{1,2,0:T(8,128)(2,1)}, u32[]{:S(2)}) copy-start(bf16[4,1024,1152]{1,2,0:T(8,128)(2,1)} %get-tuple-element.439) | copy-start | bytes 28311556 | tf_op jit(solution)/shard_map/while
  358.7 5.1 %copy-start.2 = (bf16[4,1024,1152]{1,2,0:T(8,128)(2,1)S(1)}, bf16[4,1024,1152]{1,2,0:T(8,128)(2,1)}, u32[]{:S(2)}) copy-start(bf16[4,1024,1152]{1,2,0:T(8,128)(2,1)} %get-tuple-element.439) | copy-start | bytes 28311556 | tf_op jit(solution)/shard_map/while
  374.9 5.1 %copy-start.2 = (bf16[4,1024,1152]{1,2,0:T(8,128)(2,1)S(1)}, bf16[4,1024,1152]{1,2,0:T(8,128)(2,1)}, u32[]{:S(2)}) copy-start(bf16[4,1024,1152]{1,2,0:T(8,128)(2,1)} %get-tuple-element.439) | copy-start | bytes 28311556 | tf_op jit(solution)/shard_map/while
  391.0 5.1 %copy-start.2 = (bf16[4,1024,1152]{1,2,0:T(8,128)(2,1)S(1)}, bf16[4,1024,1152]{1,2,0:T(8,128)(2,1)}, u32[]{:S(2)}) copy-start(bf16[4,1024,1152]{1,2,0:T(8,128)(2,1)} %get-tuple-element.439) | copy-start | bytes 28311556 | tf_op jit(solution)/shard_map/while
  407.2 5.1 %copy-start.2 = (bf16[4,1024,1152]{1,2,0:T(8,128)(2,1)S(1)}, bf16[4,1024,1152]{1,2,0:T(8,128)(2,1)}, u32[]{:S(2)}) copy-start(bf16[4,1024,1152]{1,2,0:T(8,128)(2,1)} %get-tuple-element.439) | copy-start | bytes 28311556 | tf_op jit(solution)/shard_map/while
  423.3 5.1 %copy-start.2 = (bf16[4,1024,1152]{1,2,0:T(8,128)(2,1)S(1)}, bf16[4,1024,1152]{1,2,0:T(8,128)(2,1)}, u32[]{:S(2)}) copy-start(bf16[4,1024,1152]{1,2,0:T(8,128)(2,1)} %get-tuple-element.439) | copy-start | bytes 28311556 | tf_op jit(solution)/shard_map/while
  439.5 5.1 %copy-start.2 = (bf16[4,1024,1152]{1,2,0:T(8,128)(2,1)S(1)}, bf16[4,1024,1152]{1,2,0:T(8,128)(2,1)}, u32[]{:S(2)}) copy-start(bf16[4,1024,1152]{1,2,0:T(8,128)(2,1)} %get-tuple-element.439) | copy-start | bytes 28311556 | tf_op jit(solution)/shard_map/while
  455.6 5.1 %copy-start.2 = (bf16[4,1024,1152]{1,2,0:T(8,128)(2,1)S(1)}, bf16[4,1024,1152]{1,2,0:T(8,128)(2,1)}, u32[]{:S(2)}) copy-start(bf16[4,1024,1152]{1,2,0:T(8,128)(2,1)} %get-tuple-element.439) | copy-start | bytes 28311556 | tf_op jit(solution)/shard_map/while
  (1 other events, 2.1 us)
Sparse Core Ops, SparseCore 0:
  39.8 293.6 all-gather.2
where the time goes:
time: 480 us; the launch traced here: 478 us
  waiting for transfers between devices  243 us (51%)
  local copies, waits for them, and re-layouts  90.3 us (19%)
  matrix products  63.8 us (13%)
  other arithmetic  26.1 us (5%)
  blocking collectives  21.2 us (4%)
  starting transfers between devices  18.3 us (4%)
  between operations  14.3 us (3%)
    all_gather x1, waiting for transfers between devices, body(): far_keys = lax.all_gather(col_done, 'row', axis=1, tiled=True)  228 us
    slice x16, local copies, waits for them, and re-layouts, pair_step(): valtan_parts.append(columns(block[3]).reshape(count, 2, head_dim))  30.8 us
    unnamed x25, local copies, waits for them, and re-layouts  23.5 us
    all_gather x1, blocking collectives, body(): col_done = lax.all_gather(far_local, 'col', axis=1, tiled=True)  21.2 us
    dot_general x24, matrix products, pair_step(): jnp.einsum('qhd,khd->hqk', query_pair, keytan_part, preferred_element_typ...  14.7 us
    concatenate x2, other arithmetic, with_halo(): jnp.concatenate([lax.ppermute(tail, axis, [(i, (i + 1) % count) for i in...  12.6 us
    dynamic_slice x112, local copies, waits for them, and re-layouts, columns(): return lax.dynamic_slice_in_dim(array, start, pair_width, array.ndim - 1)  11.6 us
    while x16, local copies, waits for them, and re-layouts  11 us
  transfers between devices with their start and end apart: 7, of which 6 were waited for; matrix products, arithmetic and copies ran while one was open for 8% of the time, Pallas kernels for 0%

commit v1 on v0

--- a/solution.py
+++ b/solution.py
@@ -69,7 +69,9 @@
     near_keys = jnp.concatenate([near_pair, partner(near_pair, "col", 0)], axis=1)
     far_local = pool_stack(stacked_wide, pool_far, window)
     col_done = lax.all_gather(far_local, "col", axis=1, tiled=True)
-    far_keys = lax.all_gather(col_done, "row", axis=1, tiled=True)
+    far_keys = jnp.concatenate(
+        lax.all_to_all(jnp.stack([col_done] * lax.axis_size("row")), "row", 0, 0), axis=1
+    )
     row_ids = lax.axis_index("row") * window - RIM + jnp.arange(span, dtype=jnp.int32)
     col_ids = lax.axis_index("col") * window - RIM + jnp.arange(span, dtype=jnp.int32)
     row_ok = (row_ids >= 0) & (row_ids < window * lax.axis_size("row"))

time: 480 us -> 576 us (1.20)
  the two profiles are of different devices: /device:TPU:96 before, /device:TPU:137 now
where the time goes in v1:
time: 576 us; the launch traced here: 575 us
  starting transfers between devices  249 us (43%)
  waiting for transfers between devices  110 us (19%)
  local copies, waits for them, and re-layouts  105 us (18%)
  matrix products  64.1 us (11%)
  other arithmetic  24.1 us (4%)
  blocking collectives  20.2 us (4%)
    ppermute x2, starting transfers between devices, with_halo(): lax.ppermute(tail, axis, [(i, (i + 1) % count) for i in range(ends)])  216 us
    ppermute x2, waiting for transfers between devices, with_halo(): lax.ppermute(tail, axis, [(i, (i + 1) % count) for i in range(ends)])  96.5 us
    slice x16, local copies, waits for them, and re-layouts, pair_step(): valtan_parts.append(columns(block[3]).reshape(count, 2, head_dim))  30.8 us
    unnamed x31, local copies, waits for them, and re-layouts  23.6 us
    all_gather x1, blocking collectives, body(): col_done = lax.all_gather(far_local, 'col', axis=1, tiled=True)  20.2 us
    dynamic_slice x112, local copies, waits for them, and re-layouts, columns(): return lax.dynamic_slice_in_dim(array, start, pair_width, array.ndim - 1)  18.7 us
    ppermute x2, starting transfers between devices, with_halo(): lax.ppermute(head, axis, [((i + 1) % count, i) for i in range(ends)])  15.8 us
    dot_general x24, matrix products, pair_step(): jnp.einsum('qhd,khd->hqk', query_pair, keytan_part, preferred_element_typ...  14.7 us
  transfers between devices with their start and end apart: 7, of which 5 were waited for; matrix products, arithmetic and copies ran while one was open for 6% of the time, Pallas kernels for 0%

profile of v1, /device:TPU:137, one launch (start us, length us, event | category | flops | bytes accessed | tf_op | source)
XLA Modules:
  0.0 574.7 jit_solution(12442402790773903179)
XLA Ops:
  3.7 20.2 %all-gather = bf16[4,18432]{1,0:T(4,128)(2,1)S(1)} all-gather(bf16[4,1152]{1,0:T(4,128)(2,1)S(1)} %bitcast.214), channel_id=2, replica_groups=mesh['row'=32,'col'=16] {'col'}, dimensions={1}, use_global_device_ids=true | all-gather | bytes 156672 | tf_op jit(solution)/shard_map/all_gather | solution.py:71
  26.7 12.8 %all-to-all-start = ((bf16[32,4,16,1152]{3,2,1,0:T(8,128)(2,1)}), bf16[32,4,16,1152]{3,2,1,0:T(8,128)(2,1)}, u32[]{:S(2)}, u32[]{:S(2)}) async-start(bf16[32,4,16,1152]{3,2,1,0:T(8,128)(2,1)} %stack.32), calls=%async_computation | async-start | bytes 9437184 | tf_op jit(solution)/shard_map/all_to_all | solution.py:73
  39.8 3.2 collective-permute-start
  43.0 13.9 %collective-permute-start.1 = (bf16[4,8,16,1152]{3,2,1,0:T(8,128)(2,1)S(1)}, bf16[4,8,16,1152]{3,2,1,0:T(8,128)(2,1)S(1)}, u32[]{:S(2)}, u32[]{:S(2)}) collective-permute-start(bf16[4,8,16,1152]{3,2,1,0:T(8,128)(2,1)S(1)} %get-tuple-element.277), channel_id=1, source_target_pairs={{16,0},{32,16},{48,32},{64,48},{80,64},{96,80},{112,96},{128,112},... | collective-permute-start | bytes 3538952 | tf_op jit(solution)/shard_map/ppermute | solution.py:21
  56.9 91.9 %collective-permute-done = bf16[4,8,16,1152]{3,2,1,0:T(8,128)(2,1)S(1)} collective-permute-done((bf16[4,8,16,1152]{3,2,1,0:T(8,128)(2,1)S(1)}, bf16[4,8,16,1152]{3,2,1,0:T(8,128)(2,1)S(1)}, u32[]{:S(2)}, u32[]{:S(2)}) %collective-permute-start) | collective-permute-done | bytes 1179680 | tf_op jit(solution)/shard_map/ppermute | solution.py:19
  148.8 5.1 collective-permute-done.1
  158.5 213.0 %collective-permute-start.2 = (bf16[4,32,8,1152]{3,2,1,0:T(8,128)(2,1)}, bf16[4,32,8,1152]{3,2,1,0:T(8,128)(2,1)}, u32[]{:S(2)}, u32[]{:S(2)}) collective-permute-start(bf16[4,32,8,1152]{3,2,1,0:T(8,128)(2,1)} %get-tuple-element.274), channel_id=1, source_target_pairs={{0,1},{1,2},{2,3},{3,4},{4,5},{5,6},{6,7},{7,8},{8,9},{9,10},{10,1... | collective-permute-start | bytes 7077896 | tf_op jit(solution)/shard_map/ppermute | solution.py:19
  376.5 3.7 fusion.44
  382.3 4.4 collective-permute-done.4
  393.1 4.6 collective-permute-done.2
  397.6 4.4 collective-permute-done.3
  402.0 9.9 %pad_maximum_fusion = bf16[4,32,32,1152]{3,2,1,0:T(8,128)(2,1)} fusion(bf16[4,32,8,1152]{3,2,1,0:T(8,128)(2,1)} %collective-permute-done.3, bf16[4,8,16,1152]{3,2,1,0:T(8,128)(2,1)} %copy-done.10, bf16[1,16,16,1152]{3,2,1,0:T(8,128)(2,1)S(1)} %bitcast.192, bf16[1,16,16,1152]{3,2,1,0:T(8,128)(2,1)S(1)} %bitcast.195, ...), kind=kLoop, calls=%fused_computation.75 | loop fusion | flops 75497472 | bytes 18874368 | tf_op jit(solution)/shard_map/concatenate | solution.py:17
  411.9 12.7 %copy.35 = bf16[4,1024,1152]{1,2,0:T(8,128)(2,1)} copy(bf16[4,1024,1152]{2,1,0:T(8,128)(2,1)} %bitcast.172) | data formatting | bytes 18874368
  424.6 4.9 copy.34
  429.5 6.7 %copy.37 = bf16[4,512,1152]{1,2,0:T(8,128)(2,1)} copy(bf16[4,512,1152]{2,1,0:T(8,128)(2,1)} %bitcast.188) | data formatting | bytes 9437184
  436.2 136.3 %while.16 = (s32[]{:T(128)}, bf16[256,1152]{0,1:T(8,128)(2,1)S(1)}, bf16[256,1152]{0,1:T(8,128)(2,1)S(1)}, bf16[4,1024,1152]{1,2,0:T(8,128)(2,1)}, bf16[256,1152...) while((s32[]{:T(128)}, bf16[256,1152]{0,1:T(8,128)(2,1)S(1)}, ...), condition=%wide.region_10.11_spmd.clone, body=%wide.region_0.10_spmd.clone.sunk | while | flops 726347264 | bytes 104430016 | solution.py:158
  439.4 2.8 fusion.181
  456.4 2.8 fusion.181
  473.5 2.8 fusion.181
  490.5 2.8 fusion.181
  507.5 2.8 fusion.181
  524.6 2.8 fusion.181
  541.6 2.8 fusion.181
  558.7 2.8 fusion.181
  (470 shorter events, 138.4 us)
Async XLA Ops:
  26.7 397.8 %all-to-all-start = ((bf16[32,4,16,1152]{3,2,1,0:T(8,128)(2,1)}), bf16[32,4,16,1152]{3,2,1,0:T(8,128)(2,1)}, u32[]{:S(2)}, u32[]{:S(2)}) async-start(bf16[32,4,16,1152]{3,2,1,0:T(8,128)(2,1)} %stack.32), calls=%async_computation | async-start | bytes 9437184 | tf_op jit(solution)/shard_map/all_to_all | solution.py:73
  39.5 115.4 %copy-start.3 = (bf16[16,16,1152]{2,1,0:T(8,128)(2,1)S(1)}, bf16[16,16,1152]{2,1,0:T(8,128)(2,1)}, u32[]{:S(2)}) copy-start(bf16[16,16,1152]{2,1,0:T(8,128)(2,1)} %param.16) | copy-start | bytes 1769476
  39.5 115.4 %copy-start.4 = (bf16[16,16,1152]{2,1,0:T(8,128)(2,1)S(1)}, bf16[16,16,1152]{2,1,0:T(8,128)(2,1)}, u32[]{:S(2)}) copy-start(bf16[16,16,1152]{2,1,0:T(8,128)(2,1)} %param.15) | copy-start | bytes 1769476
  39.6 115.4 %copy-start.5 = (bf16[16,16,1152]{2,1,0:T(8,128)(2,1)S(1)}, bf16[16,16,1152]{2,1,0:T(8,128)(2,1)}, u32[]{:S(2)}) copy-start(bf16[16,16,1152]{2,1,0:T(8,128)(2,1)} %param.13) | copy-start | bytes 1769476
  39.6 115.4 %copy-start.7 = (bf16[16,16,1152]{2,1,0:T(8,128)(2,1)S(1)}, bf16[16,16,1152]{2,1,0:T(8,128)(2,1)}, u32[]{:S(2)}) copy-start(bf16[16,16,1152]{2,1,0:T(8,128)(2,1)} %param.12) | copy-start | bytes 1769476
  39.8 109.1 %collective-permute-start = (bf16[4,8,16,1152]{3,2,1,0:T(8,128)(2,1)S(1)}, bf16[4,8,16,1152]{3,2,1,0:T(8,128)(2,1)S(1)}, u32[]{:S(2)}, u32[]{:S(2)}) collective-permute-start(bf16[4,8,16,1152]{3,2,1,0:T(8,128)(2,1)S(1)} %get-tuple-element.276), channel_id=1, source_target_pairs={{0,16},{16,32},{32,48},{48,64},{64,80},{80,96},{96,112},{112,128},... | collective-permute-start | bytes 3538952 | tf_op jit(solution)/shard_map/ppermute | solution.py:19
  43.0 110.9 %collective-permute-start.1 = (bf16[4,8,16,1152]{3,2,1,0:T(8,128)(2,1)S(1)}, bf16[4,8,16,1152]{3,2,1,0:T(8,128)(2,1)S(1)}, u32[]{:S(2)}, u32[]{:S(2)}) collective-permute-start(bf16[4,8,16,1152]{3,2,1,0:T(8,128)(2,1)S(1)} %get-tuple-element.277), channel_id=1, source_target_pairs={{16,0},{32,16},{48,32},{64,48},{80,64},{96,80},{112,96},{128,112},... | collective-permute-start | bytes 3538952 | tf_op jit(solution)/shard_map/ppermute | solution.py:21
  148.8 5.1 copy-start.9
  155.9 217.6 %copy-start.8 = (bf16[16,16,1152]{2,1,0:T(8,128)(2,1)S(1)}, bf16[16,16,1152]{2,1,0:T(8,128)(2,1)}, u32[]{:S(2)}) copy-start(bf16[16,16,1152]{2,1,0:T(8,128)(2,1)} %param.12) | copy-start | bytes 1769476
  155.9 217.8 %copy-start.6 = (bf16[16,16,1152]{2,1,0:T(8,128)(2,1)S(1)}, bf16[16,16,1152]{2,1,0:T(8,128)(2,1)}, u32[]{:S(2)}) copy-start(bf16[16,16,1152]{2,1,0:T(8,128)(2,1)} %param.13) | copy-start | bytes 1769476
  158.5 239.1 %collective-permute-start.2 = (bf16[4,32,8,1152]{3,2,1,0:T(8,128)(2,1)}, bf16[4,32,8,1152]{3,2,1,0:T(8,128)(2,1)}, u32[]{:S(2)}, u32[]{:S(2)}) collective-permute-start(bf16[4,32,8,1152]{3,2,1,0:T(8,128)(2,1)} %get-tuple-element.274), channel_id=1, source_target_pairs={{0,1},{1,2},{2,3},{3,4},{4,5},{5,6},{6,7},{7,8},{8,9},{9,10},{10,1... | collective-permute-start | bytes 7077896 | tf_op jit(solution)/shard_map/ppermute | solution.py:19
  371.5 30.5 %collective-permute-start.3 = (bf16[4,32,8,1152]{3,2,1,0:T(8,128)(2,1)}, bf16[4,32,8,1152]{3,2,1,0:T(8,128)(2,1)}, u32[]{:S(2)}, u32[]{:S(2)}) collective-permute-start(bf16[4,32,8,1152]{3,2,1,0:T(8,128)(2,1)} %get-tuple-element.275), channel_id=1, source_target_pairs={{1,0},{2,1},{3,2},{4,3},{5,4},{6,5},{7,6},{8,7},{9,8},{10,9},{11,1... | collective-permute-start | bytes 7077896 | tf_op jit(solution)/shard_map/ppermute | solution.py:21
  376.5 12.3 %copy-start.11 = (bf16[16,16,1152]{2,1,0:T(8,128)(2,1)S(1)}, bf16[16,16,1152]{2,1,0:T(8,128)(2,1)}, u32[]{:S(2)}) copy-start(bf16[16,16,1152]{2,1,0:T(8,128)(2,1)} %param.11) | copy-start | bytes 1769476
  380.4 6.3 %collective-permute-start.4 = (bf16[4,16,1152]{2,1,0:T(8,128)(2,1)S(1)}, bf16[4,16,1152]{2,1,0:T(8,128)(2,1)S(1)}, u32[]{:S(2)}, u32[]{:S(2)}) collective-permute-start(bf16[4,16,1152]{2,1,0:T(8,128)(2,1)S(1)} %reshape.234), channel_id=1, source_target_pairs={{0,16},{16,0},{32,48},{48,32},{64,80},{80,64},{96,112},{112,96},{1... | collective-permute-start | bytes 442376 | tf_op jit(solution)/shard_map/ppermute | solution.py:35
  386.7 5.3 collective-permute-start.5
  429.4 6.8 %copy-start.12 = (f32[2,16]{1,0:T(2,128)S(1)}, f32[2,16]{1,0:T(2,128)}, u32[]{:S(2)}) copy-start(f32[2,16]{1,0:T(2,128)} %param.19) | copy-start | bytes 388
  439.4 5.1 copy-start.2
  456.4 5.1 copy-start.2
  473.5 5.1 copy-start.2
  490.5 5.1 copy-start.2
  507.5 5.1 copy-start.2
  524.6 5.1 copy-start.2
  541.6 5.1 copy-start.2
  558.7 5.1 copy-start.2
  (4 other events, 10.1 us)
